TPU v7x, 512 devices: a whole 4x8x8 slice. The times are simulated.
512 devices in a mesh: seq: 128 (over z, y, core), tp: 4 (over x).
Axes of the slice: x: 4, y: 8, z: 8, core: 2. Of those that a mesh axis runs over, the one named last changes fastest.
Arguments:
- queries: bfloat16 [32768, 4096], P('seq', 'tp'), may hold values from -6 to 6, as said below
- keys: bfloat16 [32768, 512], P('seq', 'tp'), may hold values from -6 to 6, as said below
- values: bfloat16 [32768, 512], P('seq', 'tp'), may hold values from -6 to 6
- segment: int32 [32768], P('seq'), may hold values from 0 to 255, never falling along the last dimension, each value on 1 to 512 neighbouring positions
- repack: int32 [32768], P('seq'), may hold values from 0 to 32767, as said below
- proj: bfloat16 [1536, 4096], P('seq', 'tp'), may hold values from -0.5 to 0.5
- student_states: bfloat16 [32768, 1536], P('seq'), may hold values from -6 to 6
- target_row: int32 [32768], P('seq'), may hold values from 0 to 255
Outputs:
- student_rows: bfloat16 [32768, 1536], P('seq', 'tp')
- grad: float32 [1536, 4096], P('seq', 'tp')
Inputs may be any that keep to these rules, and one draw needn't show every extreme that they name: `queries`: scaled normal entries. `keys`: scaled normal entries. `repack`: A permutation of the student rows. Each device's teacher rows go in consecutive groups of 4 rows, in order, each group to one student owner (the device holding student rows owner * 256 to owner * 256 + 255); every device sends exactly 4 rows to each of 64 other devices and none to itself, so at most 4 rows from one device to one owner, reached by every sending pair.
All inputs are finite; a program needn't handle non-finite values.
Results may differ from a plain program's by a relative error of at most 0.0056.
Values may be sent and summed in bfloat16 or wider, within the bound.
No kernel may reach another device: no remote copies, remote signals or barrier semaphores. Data moves between devices by JAX's collectives and lax.ppermute only.
A program may use at most 64 MiB of HBM per device.

v0:
```python
import math
import jax
import jax.numpy as jnp
from jax import lax
from jax.sharding import PartitionSpec as P

HEADS = 32
KV_HEADS = 4
HEAD_DIM = 128
SW = 1536
REACH = 2
GROUP_ROWS = 4
neg_large = -1e30


def passed_along(block, axis, distance):
    devices = range(lax.axis_size(axis))
    route = [(i - distance, i) for i in devices if i - distance in devices]
    return lax.ppermute(block, axis, route)


def attend(queries, keys, values, segment):
    row_count = queries.shape[0]
    lanes = keys.shape[1]
    seg_rows = (segment + 1).astype(jnp.bfloat16).reshape(-1, lanes)
    seg_rows = jnp.concatenate([seg_rows, jnp.zeros((14, lanes), jnp.bfloat16)], 0)
    packed = jnp.concatenate([keys, values, seg_rows], 0)
    blocks = [packed]
    for step in range(1, REACH + 1):
        blocks.insert(0, passed_along(packed, "seq", step))
    all_keys = jnp.concatenate([b[:row_count] for b in blocks], 0)
    all_values = jnp.concatenate([b[row_count : 2 * row_count] for b in blocks], 0)
    key_seg = jnp.concatenate(
        [b[2 * row_count : 2 * row_count + 2].reshape(-1) for b in blocks], 0
    ).astype(jnp.int32)
    key_pos = jnp.arange(3 * row_count, dtype=jnp.int32) - REACH * row_count
    row_pos = jnp.arange(row_count, dtype=jnp.int32)
    allowed = (key_seg[None, :] == (segment + 1)[:, None]) & (key_pos[None, :] <= row_pos[:, None])
    group = HEADS // KV_HEADS
    q_heads = queries.reshape(row_count, group, HEAD_DIM)
    scale = 1.0 / math.sqrt(HEAD_DIM)
    outputs = []
    for head in range(group):
        scores = (
            jnp.einsum("td,sd->ts", q_heads[:, head], all_keys, preferred_element_type=jnp.float32)
            * scale
        )
        scores = jnp.where(allowed, scores, neg_large)
        top = jnp.max(scores, axis=-1, keepdims=True)
        expo = jnp.exp(scores - top)
        weights = (expo / jnp.sum(expo, axis=-1, keepdims=True)).astype(jnp.bfloat16)
        mixed = jnp.einsum("ts,sd->td", weights, all_values, preferred_element_type=jnp.float32)
        outputs.append(mixed.astype(jnp.bfloat16))
    return jnp.concatenate(outputs, axis=1)


def on_device(queries, keys, values, segment, repack, proj, student_states, target_row):
    row_count = queries.shape[0]
    devices = lax.axis_size("seq")
    groups = row_count // GROUP_ROWS
    attended = attend(queries, keys, values, segment)
    target_dev = repack // row_count
    local_slot = repack - target_dev * row_count
    owners = target_dev.reshape(groups, GROUP_ROWS)[:, 0]
    owner_hot = owners[None, :] == jnp.arange(devices, dtype=jnp.int32)[:, None]
    slots_by_group = local_slot.reshape(groups, GROUP_ROWS)
    slot_table = jnp.sum(jnp.where(owner_hot[:, :, None], slots_by_group[None], 0), axis=1)
    slot_table = jnp.where(jnp.any(owner_hot, axis=1)[:, None], slot_table, row_count)
    slots = lax.all_to_all(slot_table, "seq", split_axis=0, concat_axis=0, tiled=True)
    width_share = SW // lax.axis_size("tp")
    tp_index = lax.axis_index("tp")
    targets = student_states[target_row]
    bucket_dev = jnp.arange(devices * GROUP_ROWS, dtype=jnp.int32) // GROUP_ROWS
    bucket_pos = jnp.arange(devices * GROUP_ROWS, dtype=jnp.int32) % GROUP_ROWS
    row_ids = jnp.arange(row_count, dtype=jnp.int32)
    pick = (
        (bucket_dev[:, None] == target_dev[None, :])
        & (bucket_pos[:, None] == (row_ids % GROUP_ROWS)[None, :])
    ).astype(jnp.bfloat16)
    buckets = jnp.dot(pick, attended, preferred_element_type=jnp.float32).astype(jnp.bfloat16)
    arrived = lax.all_to_all(buckets, "seq", split_axis=0, concat_axis=0, tiled=True)
    place = (row_ids[:, None] == slots.reshape(-1)[None, :]).astype(jnp.bfloat16)
    student_x = jnp.dot(place, arrived, preferred_element_type=jnp.float32).astype(jnp.bfloat16)
    all_proj = lax.all_gather(proj, "seq", axis=0, tiled=True)
    y_part = jnp.einsum("tf,nf->tn", student_x, all_proj, preferred_element_type=jnp.float32)
    y_total = lax.psum(y_part, "tp")
    y_rounded = y_total.astype(jnp.bfloat16)
    delta = (y_rounded.astype(jnp.float32) - targets.astype(jnp.float32)).astype(jnp.bfloat16)
    out_rows = lax.dynamic_slice_in_dim(y_rounded, tp_index * width_share, width_share, 1)
    norm_factor = 1.0 / math.sqrt(row_count * devices)
    grad_rows = delta.shape[1] // devices
    term = jnp.einsum("ts,tf->sf", delta, student_x, preferred_element_type=jnp.float32)
    pieces = term.reshape(devices, grad_rows, term.shape[1])
    summed = lax.all_to_all(
        pieces.astype(jnp.bfloat16), "seq", split_axis=0, concat_axis=0, tiled=True
    ).astype(pieces.dtype)
    grad = jnp.sum(summed, axis=0) * norm_factor
    return (out_rows, grad)


def solution(mesh):
    placed = (
        P("seq", "tp"),
        P("seq", "tp"),
        P("seq", "tp"),
        P("seq"),
        P("seq"),
        P("seq", "tp"),
        P("seq", None),
        P("seq"),
    )
    return jax.shard_map(
        on_device,
        mesh=mesh,
        in_specs=placed,
        out_specs=(P("seq", "tp"), P("seq", "tp")),
        check_vma=False,
    )
```

profile of v0, /device:TPU:41, one launch (start us, length us, event | category | flops | bytes accessed | tf_op | source)
XLA Modules:
  0.0 316.8 jit_solution(7449039841433495899)
XLA Ops:
  7.2 0.0 copy-start
  7.2 0.0 copy-start.1
  7.2 0.8 broadcast_add_fusion
  8.0 0.1 pad.12.clone
  8.0 1.0 maximum_maximum_fusion
  9.1 2.9 collective-permute-start.1
  11.9 2.3 collective-permute-start
  14.2 0.7 multiply_subtract_fusion
  14.9 0.1 broadcast_in_dim.51
  15.1 0.1 copy.28
  15.1 0.1 reshape.146
  15.2 0.1 slice_reduce_fusion
  15.4 0.1 fusion.48
  15.5 0.1 select_reduce_fusion
  15.6 0.7 copy.29
  16.3 16.6 %all-to-all-start = ((s32[128,1,4]{2,1,0:T(1,128)}), s32[128,1,4]{2,1,0:T(1,128)S(1)}, u32[]{:S(2)}, u32[]{:S(2)}) async-start(s32[128,1,4]{2,1,0:T(1,128)} %copy.29), calls=%async_computation | async-start | bytes 131072 | tf_op jit(solution)/shard_map/all_to_all | solution.py:69
  33.0 0.0 all-gather.3.cloned.1.call-start
  33.0 0.7 all-gather.3.cloned.1.call-update
  33.7 1.2 copy.30
  35.1 1.2 fusion.52
  36.3 0.3 fusion.53
  36.6 0.3 fusion.54
  37.0 0.4 fusion.55
  37.3 0.2 fusion.25
  37.5 0.2 fusion.26
  37.7 0.2 fusion.27
  37.8 0.2 fusion.28
  38.0 0.3 fusion.56
  38.4 0.2 fusion.29
  38.5 0.4 fusion.57
  38.9 0.2 fusion.30
  39.1 0.3 fusion.58
  39.4 0.2 fusion.31
  39.6 0.3 fusion.59
  40.0 0.2 fusion.32
  40.1 0.3 fusion.16
  40.4 0.3 fusion.17
  40.7 0.3 fusion.18
  41.0 0.3 fusion.19
  41.3 0.3 fusion.20
  41.6 0.3 fusion.21
  41.9 0.3 fusion.22
  42.2 0.3 fusion.23
  42.6 0.5 convolution_convert_fusion.1
  43.0 1.2 all_to_all.16
  44.3 13.7 %all-to-all-start.1 = ((bf16[128,4,1024]{2,1,0:T(4,128)(2,1)}), bf16[128,4,1024]{2,1,0:T(4,128)(2,1)S(1)}, u32[]{:S(2)}, u32[]{:S(2)}) async-start(bf16[128,4,1024]{2,1,0:T(4,128)(2,1)} %all_to_all.16), calls=%async_computation.1 | async-start | bytes 2097152 | tf_op jit(solution)/shard_map/all_to_all | solution.py:81
  58.1 1.3 gather_fusion
  59.4 0.5 broadcast.182
  59.9 0.8 reduce.5
  60.7 0.1 eq.82
  60.8 26.4 %all-to-all-done.1 = bf16[128,4,1024]{2,1,0:T(4,128)(2,1)S(1)} async-done(((bf16[128,4,1024]{2,1,0:T(4,128)(2,1)}), bf16[128,4,1024]{2,1,0:T(4,128)(2,1)S(1)}, u32[]{:S(2)}, u32[]{:S(2)}) %all-to-all-start.1) | async-done | bytes 1048608 | tf_op jit(solution)/shard_map/all_to_all | solution.py:81
  87.2 1.1 all_to_all.18
  88.3 1.7 convolution_convert_fusion.2
  90.0 46.0 %all-gather.3.cloned.1.call-done = bf16[128,12,1024]{2,1,0:T(8,128)(2,1)} async-done(((bf16[1,12,1024]{2,1,0:T(8,128)(2,1)}), bf16[128,12,1024]{2,1,0:T(8,128)(2,1)}) %all-gather.3.cloned.1.call-update) | async-done | bytes 3145744 | tf_op jit(solution)/shard_map/all_gather | solution.py:84
  136.0 6.2 %reshape.159 = bf16[1536,1024]{1,0:T(8,128)(2,1)} reshape(bf16[128,12,1024]{2,1,0:T(8,128)(2,1)} %all-gather.3.cloned.1.call-done) | data formatting | bytes 6291456
  142.2 4.1 %fusion.60 = f32[256,1536]{1,0:T(8,128)} fusion(bf16[256,1024]{1,0:T(8,128)(2,1)S(1)} %convolution_convert_fusion.2, bf16[1536,1024]{1,0:T(8,128)(2,1)} %reshape.159), kind=kOutput, calls=%fused_computation.134 | convolution fusion | flops 805306368 | bytes 5242880 | tf_op jit(solution)/shard_map/tf,nf->tn/dot_general | solution.py:85
  146.2 33.8 %all-reduce.1 = bf16[256,1536]{1,0:T(8,128)(2,1)S(1)} all-reduce(f32[256,1536]{1,0:T(8,128)} %fusion.60), channel_id=1, replica_groups=mesh['seq'=128,'tp'=4] {'tp'}, use_global_device_ids=true, to_apply=%region_18.19 | all-reduce | flops 393216 | bytes 2359296 | tf_op jit(solution)/shard_map/psum | solution.py:86
  180.0 2.7 convolution_convert_fusion
  182.7 6.1 %convert_element_type.112 = bf16[128,12,1024]{2,1,0:T(8,128)(2,1)} reshape(bf16[1536,1024]{1,0:T(8,128)(2,1)} %convolution_convert_fusion) | data formatting | bytes 6291456 | tf_op jit(solution)/shard_map/convert_element_type | solution.py:95
  188.8 13.8 %all-to-all-start.2 = ((bf16[128,12,1024]{2,1,0:T(8,128)(2,1)}), bf16[128,12,1024]{2,1,0:T(8,128)(2,1)}, u32[]{:S(2)}, u32[]{:S(2)}) async-start(bf16[128,12,1024]{2,1,0:T(8,128)(2,1)} %convert_element_type.112), calls=%async_computation.2 | async-start | bytes 8388608 | tf_op jit(solution)/shard_map/all_to_all | solution.py:94
  202.6 0.7 constant_dynamic-slice_fusion
  203.3 103.0 %all-to-all-done.2 = bf16[128,12,1024]{2,1,0:T(8,128)(2,1)} async-done(((bf16[128,12,1024]{2,1,0:T(8,128)(2,1)}), bf16[128,12,1024]{2,1,0:T(8,128)(2,1)}, u32[]{:S(2)}, u32[]{:S(2)}) %all-to-all-start.2) | async-done | bytes 3145760 | tf_op jit(solution)/shard_map/all_to_all | solution.py:94
  306.3 3.0 convert_reduce_fusion
  309.3 0.6 broadcast_multiply_fusion
  (21 shorter events, 0.1 us)
Async XLA Ops:
  7.2 50.9 %copy-start = (bf16[256,1536]{1,0:T(8,128)(2,1)S(1)}, bf16[256,1536]{1,0:T(8,128)(2,1)}, u32[]{:S(2)}) copy-start(bf16[256,1536]{1,0:T(8,128)(2,1)} %param.14) | copy-start | bytes 2359300
  7.2 29.1 %copy-start.1 = (bf16[256,128]{1,0:T(8,128)(2,1)S(1)}, bf16[256,128]{1,0:T(8,128)(2,1)}, u32[]{:S(2)}) copy-start(bf16[256,128]{1,0:T(8,128)(2,1)} %param.9) | copy-start | bytes 196612
  9.1 25.9 %collective-permute-start.1 = (bf16[528,128]{1,0:T(8,128)(2,1)S(1)}, bf16[528,128]{1,0:T(8,128)(2,1)S(1)}, u32[]{:S(2)}, u32[]{:S(2)}) collective-permute-start(bf16[528,128]{1,0:T(8,128)(2,1)S(1)} %maximum_maximum_fusion), channel_id=1, source_target_pairs={{0,4},{4,8},{8,12},{12,16},{16,20},{20,24},{24,28},{28,32},{32,36}... | collective-permute-start | bytes 405512 | tf_op jit(solution)/shard_map/ppermute | solution.py:19
  11.9 23.1 %collective-permute-start = (bf16[528,128]{1,0:T(8,128)(2,1)S(1)}, bf16[528,128]{1,0:T(8,128)(2,1)S(1)}, u32[]{:S(2)}, u32[]{:S(2)}) collective-permute-start(bf16[528,128]{1,0:T(8,128)(2,1)S(1)} %maximum_maximum_fusion), channel_id=1, source_target_pairs={{0,8},{4,12},{8,16},{12,20},{16,24},{20,28},{24,32},{28,36},{32,40... | collective-permute-start | bytes 405512 | tf_op jit(solution)/shard_map/ppermute | solution.py:19
  16.3 28.0 %all-to-all-start = ((s32[128,1,4]{2,1,0:T(1,128)}), s32[128,1,4]{2,1,0:T(1,128)S(1)}, u32[]{:S(2)}, u32[]{:S(2)}) async-start(s32[128,1,4]{2,1,0:T(1,128)} %copy.29), calls=%async_computation | async-start | bytes 131072 | tf_op jit(solution)/shard_map/all_to_all | solution.py:69
  33.0 103.0 %all-gather.3.cloned.1.call-start = ((), (), s32[]{:S(2)}) async-start(), calls=%async_computation.3 | async-start | bytes 4227072 | tf_op jit(solution)/shard_map/all_gather | solution.py:84
  38.9 1.2 copy-start.2
  42.5 15.5 %copy-start.3 = (s32[256]{0:T(256)S(1)}, s32[256]{0:T(256)}, u32[]{:S(2)}) copy-start(s32[256]{0:T(256)} %param.15) | copy-start | bytes 3076
  44.3 42.9 %all-to-all-start.1 = ((bf16[128,4,1024]{2,1,0:T(4,128)(2,1)}), bf16[128,4,1024]{2,1,0:T(4,128)(2,1)S(1)}, u32[]{:S(2)}, u32[]{:S(2)}) async-start(bf16[128,4,1024]{2,1,0:T(4,128)(2,1)} %all_to_all.16), calls=%async_computation.1 | async-start | bytes 2097152 | tf_op jit(solution)/shard_map/all_to_all | solution.py:81
  188.8 117.5 %all-to-all-start.2 = ((bf16[128,12,1024]{2,1,0:T(8,128)(2,1)}), bf16[128,12,1024]{2,1,0:T(8,128)(2,1)}, u32[]{:S(2)}, u32[]{:S(2)}) async-start(bf16[128,12,1024]{2,1,0:T(8,128)(2,1)} %convert_element_type.112), calls=%async_computation.2 | async-start | bytes 8388608 | tf_op jit(solution)/shard_map/all_to_all | solution.py:94
Sparse Core Ops, SparseCore 0:
  36.9 99.0 all-gather.2
where the time goes:
time: 318 us; the launch traced here: 317 us
  waiting for transfers between devices  176 us (55%)
  starting transfers between devices  49.4 us (16%)
  blocking collectives  33.8 us (11%)
  local copies, waits for them, and re-layouts  19.7 us (6%)
  matrix products  14.9 us (5%)
  between operations  14.4 us (5%)
  other arithmetic  8.56 us (3%)
    all_to_all x1, waiting for transfers between devices, on_device(): lax.all_to_all(pieces.astype(jnp.bfloat16), 'seq', split_axis=0, concat_a...  103 us
    all_gather x1, waiting for transfers between devices, on_device(): all_proj = lax.all_gather(proj, 'seq', axis=0, tiled=True)  46 us
    psum x1, blocking collectives, on_device(): y_total = lax.psum(y_part, 'tp')  33.8 us
    all_to_all x1, waiting for transfers between devices, on_device(): lax.all_to_all(buckets, 'seq', split_axis=0, concat_axis=0, tiled=True)  26.4 us
    all_to_all x1, starting transfers between devices, on_device(): lax.all_to_all(slot_table, 'seq', split_axis=0, concat_axis=0, tiled=True)  16.6 us
    all_to_all x1, starting transfers between devices, on_device(): lax.all_to_all(pieces.astype(jnp.bfloat16), 'seq', split_axis=0, concat_a...  13.8 us
    all_to_all x1, starting transfers between devices, on_device(): lax.all_to_all(buckets, 'seq', split_axis=0, concat_axis=0, tiled=True)  13.7 us
    unnamed x10, local copies, waits for them, and re-layouts  7.43 us
  transfers between devices with their start and end apart: 6, of which 3 were waited for; matrix products, arithmetic and copies ran while one was open for 5% of the time, Pallas kernels for 0%

commit v1 on v0

--- a/solution.py
+++ b/solution.py
@@ -83,7 +83,7 @@
     student_x = jnp.dot(place, arrived, preferred_element_type=jnp.float32).astype(jnp.bfloat16)
     all_proj = lax.all_gather(proj, "seq", axis=0, tiled=True)
     y_part = jnp.einsum("tf,nf->tn", student_x, all_proj, preferred_element_type=jnp.float32)
-    y_total = lax.psum(y_part, "tp")
+    y_total = jnp.sum(lax.all_gather(y_part, "tp"), axis=0)
     y_rounded = y_total.astype(jnp.bfloat16)
     delta = (y_rounded.astype(jnp.float32) - targets.astype(jnp.float32)).astype(jnp.bfloat16)
     out_rows = lax.dynamic_slice_in_dim(y_rounded, tp_index * width_share, width_share, 1)

time: 318 us -> 357 us (1.12)
  waiting for transfers between devices: 176 us -> 245 us
  blocking collectives: 33.8 us -> 0 us
    all_gather x0 -> x1, waiting for transfers between devices: none -> 67.3 us  [on_device(): y_total = jnp.sum(lax.all_gather(y_part, 'tp'), axis=0)]
    psum x1 -> x0, blocking collectives: 33.8 us -> none  [on_device(): y_total = lax.psum(y_part, 'tp')]
  transfers between devices with their start and end apart: 6 -> 7, of which waited for: 3 -> 4; matrix products, arithmetic and copies ran while one was open for 5% -> 5% of each run, Pallas kernels for 0% -> 0%
where the time goes in v1:
time: 357 us; the launch traced here: 356 us
  waiting for transfers between devices  245 us (69%)
  starting transfers between devices  50.8 us (14%)
  local copies, waits for them, and re-layouts  19.7 us (6%)
  matrix products  14.9 us (4%)
  between operations  14.4 us (4%)
  other arithmetic  12.1 us (3%)
    all_to_all x1, waiting for transfers between devices, on_device(): lax.all_to_all(pieces.astype(jnp.bfloat16), 'seq', split_axis=0, concat_a...  103 us
    all_gather x1, waiting for transfers between devices, on_device(): y_total = jnp.sum(lax.all_gather(y_part, 'tp'), axis=0)  67.3 us
    all_gather x1, waiting for transfers between devices, on_device(): all_proj = lax.all_gather(proj, 'seq', axis=0, tiled=True)  46 us
    all_to_all x1, waiting for transfers between devices, on_device(): lax.all_to_all(buckets, 'seq', split_axis=0, concat_axis=0, tiled=True)  27.5 us
    all_to_all x1, starting transfers between devices, on_device(): lax.all_to_all(slot_table, 'seq', split_axis=0, concat_axis=0, tiled=True)  16.6 us
    all_to_all x1, starting transfers between devices, on_device(): lax.all_to_all(pieces.astype(jnp.bfloat16), 'seq', split_axis=0, concat_a...  15 us
    all_to_all x1, starting transfers between devices, on_device(): lax.all_to_all(buckets, 'seq', split_axis=0, concat_axis=0, tiled=True)  13.7 us
    unnamed x10, local copies, waits for them, and re-layouts  7.43 us
  transfers between devices with their start and end apart: 7, of which 4 were waited for; matrix products, arithmetic and copies ran while one was open for 5% of the time, Pallas kernels for 0%

profile of v1, /device:TPU:41, one launch (start us, length us, event | category | flops | bytes accessed | tf_op | source)
XLA Modules:
  0.0 356.4 jit_solution(12999609048180297622)
XLA Ops:
  7.2 0.8 broadcast_add_fusion
  8.0 0.1 pad.12.clone
  8.0 1.0 maximum_maximum_fusion
  9.1 2.9 collective-permute-start.1
  11.9 2.3 collective-permute-start
  14.2 0.7 multiply_subtract_fusion
  14.9 0.1 broadcast_in_dim.51
  15.1 0.1 copy.28
  15.1 0.1 reshape.146
  15.2 0.1 slice_reduce_fusion
  15.4 0.1 fusion.48
  15.5 0.1 select_reduce_fusion
  15.6 0.7 copy.29
  16.3 16.6 %all-to-all-start = ((s32[128,1,4]{2,1,0:T(1,128)}), s32[128,1,4]{2,1,0:T(1,128)S(1)}, u32[]{:S(2)}, u32[]{:S(2)}) async-start(s32[128,1,4]{2,1,0:T(1,128)} %copy.29), calls=%async_computation | async-start | bytes 131072 | tf_op jit(solution)/shard_map/all_to_all | solution.py:69
  33.0 0.0 all-gather.7.cloned.1.call-start
  33.0 0.7 all-gather.7.cloned.1.call-update
  33.7 1.2 copy.30
  35.1 1.2 fusion.52
  36.3 0.4 fusion.53
  36.6 0.4 fusion.54
  37.0 0.4 fusion.55
  37.3 0.2 fusion.25
  37.5 0.2 fusion.26
  37.7 0.2 fusion.27
  37.9 0.2 fusion.28
  38.0 0.4 fusion.56
  38.4 0.2 fusion.29
  38.6 0.3 fusion.57
  38.9 0.2 fusion.30
  39.1 0.3 fusion.58
  39.4 0.2 fusion.31
  39.6 0.4 fusion.59
  40.0 0.2 fusion.32
  40.2 0.3 fusion.16
  40.5 0.3 fusion.17
  40.8 0.3 fusion.18
  41.1 0.3 fusion.19
  41.4 0.3 fusion.20
  41.7 0.3 fusion.21
  42.0 0.3 fusion.22
  42.3 0.3 fusion.23
  42.6 0.5 convolution_convert_fusion.1
  43.1 1.2 all_to_all.16
  44.3 13.7 %all-to-all-start.1 = ((bf16[128,4,1024]{2,1,0:T(4,128)(2,1)}), bf16[128,4,1024]{2,1,0:T(4,128)(2,1)S(1)}, u32[]{:S(2)}, u32[]{:S(2)}) async-start(bf16[128,4,1024]{2,1,0:T(4,128)(2,1)} %all_to_all.16), calls=%async_computation.1 | async-start | bytes 2097152 | tf_op jit(solution)/shard_map/all_to_all | solution.py:81
  58.0 0.2 all-gather.5.cloned.1.call-start
  58.3 0.5 broadcast.182
  58.8 0.8 reduce.5
  59.6 0.1 eq.82
  59.7 27.5 %all-to-all-done.1 = bf16[128,4,1024]{2,1,0:T(4,128)(2,1)S(1)} async-done(((bf16[128,4,1024]{2,1,0:T(4,128)(2,1)}), bf16[128,4,1024]{2,1,0:T(4,128)(2,1)S(1)}, u32[]{:S(2)}, u32[]{:S(2)}) %all-to-all-start.1) | async-done | bytes 1048608 | tf_op jit(solution)/shard_map/all_to_all | solution.py:81
  87.2 1.1 all_to_all.18
  88.3 1.7 convolution_convert_fusion.2
  90.0 46.0 %all-gather.7.cloned.1.call-done = bf16[128,12,1024]{2,1,0:T(8,128)(2,1)} async-done(((bf16[1,12,1024]{2,1,0:T(8,128)(2,1)}), bf16[128,12,1024]{2,1,0:T(8,128)(2,1)}) %all-gather.7.cloned.1.call-update) | async-done | bytes 3145744 | tf_op jit(solution)/shard_map/all_gather | solution.py:84
  136.0 6.2 %reshape.160 = bf16[1536,1024]{1,0:T(8,128)(2,1)} reshape(bf16[128,12,1024]{2,1,0:T(8,128)(2,1)} %all-gather.7.cloned.1.call-done) | data formatting | bytes 6291456
  142.2 4.1 %fusion.60 = f32[256,1536]{1,0:T(8,128)} fusion(bf16[256,1024]{1,0:T(8,128)(2,1)S(1)} %convolution_convert_fusion.2, bf16[1536,1024]{1,0:T(8,128)(2,1)} %reshape.160), kind=kOutput, calls=%fused_computation.134 | convolution fusion | flops 805306368 | bytes 5242880 | tf_op jit(solution)/shard_map/tf,nf->tn/dot_general | solution.py:85
  146.3 1.3 gather_fusion
  147.6 67.3 %all-gather.5.cloned.1.call-done = f32[1024,1536]{1,0:T(8,128)} async-done(((f32[256,1536]{1,0:T(8,128)}), f32[1024,1536]{1,0:T(8,128)}) %all-gather.5.cloned.1.call-update) | async-done | bytes 6291472 | tf_op jit(solution)/shard_map/all_gather | solution.py:86
  214.9 3.5 reduce_sum.111
  218.4 2.7 convolution_convert_fusion
  221.1 6.1 %convert_element_type.112 = bf16[128,12,1024]{2,1,0:T(8,128)(2,1)} reshape(bf16[1536,1024]{1,0:T(8,128)(2,1)} %convolution_convert_fusion) | data formatting | bytes 6291456 | tf_op jit(solution)/shard_map/convert_element_type | solution.py:95
  227.2 15.0 %all-to-all-start.2 = ((bf16[128,12,1024]{2,1,0:T(8,128)(2,1)}), bf16[128,12,1024]{2,1,0:T(8,128)(2,1)}, u32[]{:S(2)}, u32[]{:S(2)}) async-start(bf16[128,12,1024]{2,1,0:T(8,128)(2,1)} %convert_element_type.112), calls=%async_computation.2 | async-start | bytes 8388608 | tf_op jit(solution)/shard_map/all_to_all | solution.py:94
  242.2 0.7 constant_dynamic-slice_fusion
  242.9 103.0 %all-to-all-done.2 = bf16[128,12,1024]{2,1,0:T(8,128)(2,1)} async-done(((bf16[128,12,1024]{2,1,0:T(8,128)(2,1)}), bf16[128,12,1024]{2,1,0:T(8,128)(2,1)}, u32[]{:S(2)}, u32[]{:S(2)}) %all-to-all-start.2) | async-done | bytes 3145760 | tf_op jit(solution)/shard_map/all_to_all | solution.py:94
  345.9 3.0 convert_reduce_fusion
  348.9 0.6 broadcast_multiply_fusion
  (24 shorter events, 0.1 us)
Async XLA Ops:
  7.2 139.1 %copy-start = (bf16[256,1536]{1,0:T(8,128)(2,1)S(1)}, bf16[256,1536]{1,0:T(8,128)(2,1)}, u32[]{:S(2)}) copy-start(bf16[256,1536]{1,0:T(8,128)(2,1)} %param.14) | copy-start | bytes 2359300
  7.2 29.1 %copy-start.1 = (bf16[256,128]{1,0:T(8,128)(2,1)S(1)}, bf16[256,128]{1,0:T(8,128)(2,1)}, u32[]{:S(2)}) copy-start(bf16[256,128]{1,0:T(8,128)(2,1)} %param.9) | copy-start | bytes 196612
  9.1 25.9 %collective-permute-start.1 = (bf16[528,128]{1,0:T(8,128)(2,1)S(1)}, bf16[528,128]{1,0:T(8,128)(2,1)S(1)}, u32[]{:S(2)}, u32[]{:S(2)}) collective-permute-start(bf16[528,128]{1,0:T(8,128)(2,1)S(1)} %maximum_maximum_fusion), channel_id=1, source_target_pairs={{0,4},{4,8},{8,12},{12,16},{16,20},{20,24},{24,28},{28,32},{32,36}... | collective-permute-start | bytes 405512 | tf_op jit(solution)/shard_map/ppermute | solution.py:19
  11.9 23.1 %collective-permute-start = (bf16[528,128]{1,0:T(8,128)(2,1)S(1)}, bf16[528,128]{1,0:T(8,128)(2,1)S(1)}, u32[]{:S(2)}, u32[]{:S(2)}) collective-permute-start(bf16[528,128]{1,0:T(8,128)(2,1)S(1)} %maximum_maximum_fusion), channel_id=1, source_target_pairs={{0,8},{4,12},{8,16},{12,20},{16,24},{20,28},{24,32},{28,36},{32,40... | collective-permute-start | bytes 405512 | tf_op jit(solution)/shard_map/ppermute | solution.py:19
  16.3 28.0 %all-to-all-start = ((s32[128,1,4]{2,1,0:T(1,128)}), s32[128,1,4]{2,1,0:T(1,128)S(1)}, u32[]{:S(2)}, u32[]{:S(2)}) async-start(s32[128,1,4]{2,1,0:T(1,128)} %copy.29), calls=%async_computation | async-start | bytes 131072 | tf_op jit(solution)/shard_map/all_to_all | solution.py:69
  33.0 103.0 %all-gather.7.cloned.1.call-start = ((), (), s32[]{:S(2)}) async-start(), calls=%async_computation.4 | async-start | bytes 4227072 | tf_op jit(solution)/shard_map/all_gather | solution.py:84
  38.9 1.2 copy-start.2
  44.3 42.9 %all-to-all-start.1 = ((bf16[128,4,1024]{2,1,0:T(4,128)(2,1)}), bf16[128,4,1024]{2,1,0:T(4,128)(2,1)S(1)}, u32[]{:S(2)}, u32[]{:S(2)}) async-start(bf16[128,4,1024]{2,1,0:T(4,128)(2,1)} %all_to_all.16), calls=%async_computation.1 | async-start | bytes 2097152 | tf_op jit(solution)/shard_map/all_to_all | solution.py:81
  58.0 156.8 %all-gather.5.cloned.1.call-start = ((), (), s32[]{:S(2)}) async-start(), calls=%async_computation.3 | async-start | bytes 7864320 | tf_op jit(solution)/shard_map/all_gather | solution.py:86
  142.2 4.1 %copy-start.3 = (s32[256]{0:T(256)S(1)}, s32[256]{0:T(256)}, u32[]{:S(2)}) copy-start(s32[256]{0:T(256)} %param.15) | copy-start | bytes 3076
  227.2 118.7 %all-to-all-start.2 = ((bf16[128,12,1024]{2,1,0:T(8,128)(2,1)}), bf16[128,12,1024]{2,1,0:T(8,128)(2,1)}, u32[]{:S(2)}, u32[]{:S(2)}) async-start(bf16[128,12,1024]{2,1,0:T(8,128)(2,1)} %convert_element_type.112), calls=%async_computation.2 | async-start | bytes 8388608 | tf_op jit(solution)/shard_map/all_to_all | solution.py:94
Sparse Core Ops, SparseCore 0:
  36.9 99.0 all-gather.6
  146.4 68.4 all-gather.4
